TPU v7x, 512 devices: a whole 4x8x8 slice. The times are simulated.
512 devices in a mesh: chan: 8 (over z), tm: 64 (over x, y, core).
Axes of the slice: x: 4, y: 8, z: 8, core: 2. Of those that a mesh axis runs over, the one named last changes fastest.
Arguments:
- voltages: bfloat16 [8, 2, 128, 131072], P(None, None, 'chan', 'tm'), may hold values from -100 to 100
- prototype: float32 [64], replicated, may hold values from -5 to 5
- forget: float32 [8], P('chan'), may hold values from 0.5 to 16
Outputs:
- whitened: bfloat16 [8, 256, 131072], P('chan', None, 'tm')
All inputs are finite; a program needn't handle non-finite values.
Results may differ from a plain program's by a relative error of at most 0.0071.
Values may be sent and summed in bfloat16 or wider, within the bound.
No kernel may reach another device: no remote copies, remote signals or barrier semaphores. Data moves between devices by JAX's collectives and lax.ppermute only.
A program may use at most 64 MiB of HBM per device.

v0:
```python
import math
import jax
import jax.numpy as jnp
from jax import lax
from jax.sharding import PartitionSpec as P


def passed_along(value, axis, steps):
    count = lax.axis_size(axis)
    leading, last = (max(0, -steps), min(count, count - steps))
    return lax.ppermute(value, axis, [(source, source + steps) for source in range(leading, last)])


def carried_in(value, axis, join, neutral):
    count, mine = (lax.axis_size(axis), lax.axis_index(axis))
    pieces = jax.tree.map(lambda part: lax.all_gather(part, axis), value)
    total = jax.tree.map(
        lambda part, zero: jnp.full_like(part, 0) + jnp.asarray(zero, part.dtype), value, neutral
    )

    def hop(position, total):
        longer = join(total, jax.tree.map(lambda part: part[position], pieces))
        return jax.tree.map(lambda new, old: jnp.where(position < mine, new, old), longer, total)

    return lax.fori_loop(0, count - 1, hop, total)


def coefficient_table(prototype, tap_count, filter_branches):
    shaped = prototype.reshape(tap_count, filter_branches)
    steps_p = jnp.arange(filter_branches, dtype=jnp.float32)
    phase = 2.0 * math.pi / filter_branches * (steps_p[:, None] * steps_p[None, :])
    cosine = jnp.cos(phase)
    sine = jnp.sin(phase)
    pattern = jnp.stack([jnp.stack([cosine, -sine], -1), jnp.stack([sine, cosine], -1)], axis=1)
    return (shaped[:, :, None, None, None] * pattern[None]).astype(jnp.bfloat16)


def combine_stats(earlier, later):
    gram_e, count_e, retain_e = earlier
    gram_l, count_l, retain_l = later
    return (
        gram_e * retain_l[:, None, None] + gram_l,
        count_e * retain_l + count_l,
        retain_e * retain_l,
    )


def per_device(voltages, prototype, forget):
    filter_branches = voltages.shape[0]
    local_antenna_count = voltages.shape[2]
    frame_rows = voltages.shape[3]
    tap_count = prototype.shape[0] // filter_branches
    coef_table = coefficient_table(prototype, tap_count, filter_branches)
    tail_rows = passed_along(voltages[..., frame_rows - (tap_count - 1) :], "tm", 1)
    extended = jnp.concatenate([tail_rows, voltages], axis=3)
    branch_sum = jnp.zeros((filter_branches, local_antenna_count, 2, frame_rows), jnp.float32)
    for tap_idx in range(tap_count):
        branch_sum = branch_sum + jnp.einsum(
            "pcaf,pckq->kaqf",
            extended[..., tap_idx : tap_idx + frame_rows],
            coef_table[tap_idx],
            preferred_element_type=jnp.float32,
        )
    spectrum_rows = branch_sum.reshape(filter_branches, local_antenna_count * 2, frame_rows).astype(
        jnp.bfloat16
    )
    turned = lax.all_to_all(spectrum_rows, "chan", split_axis=0, concat_axis=1, tiled=True)
    channels_per_device = turned.shape[0]
    col_count = turned.shape[1]
    gram_now = jnp.einsum("cif,cjf->cij", turned, turned, preferred_element_type=jnp.float32)
    retain = jnp.exp(-forget / lax.axis_size("tm"))
    row_count = jnp.full((channels_per_device,), float(frame_rows), jnp.float32)
    zero_count = jnp.zeros((channels_per_device,), jnp.float32)
    unit_retain = jnp.ones((channels_per_device,), jnp.float32)
    prior_gram, prior_count, unused_retain = carried_in(
        (gram_now, row_count, retain),
        "tm",
        combine_stats,
        (jnp.zeros_like(gram_now), zero_count, unit_retain),
    )
    moment = retain[:, None, None] * prior_gram + gram_now
    weight_sum = retain * prior_count + jnp.float32(frame_rows)
    factor_low = jnp.linalg.cholesky(moment / weight_sum[:, None, None])
    identity_m = jnp.broadcast_to(jnp.eye(col_count, dtype=jnp.float32), factor_low.shape)
    inverse = lax.linalg.triangular_solve(factor_low, identity_m, left_side=True, lower=True)
    whitened = jnp.einsum(
        "cij,cjf->cif", inverse, turned.astype(jnp.float32), precision=lax.Precision.HIGHEST
    )
    return whitened.astype(jnp.bfloat16)


def solution(mesh):
    placed = (P(None, None, "chan", "tm"), P(), P("chan"))
    return jax.shard_map(
        per_device, mesh=mesh, in_specs=placed, out_specs=P("chan", None, "tm"), check_vma=False
    )
```

profile of v0, /device:TPU:1, one launch (start us, length us, event | category | flops | bytes accessed | tf_op | source)
XLA Modules:
  0.0 499.1 jit_solution(7681647442495996566)
XLA Ops:
  6.5 1.9 copy.32
  8.5 4.6 collective-permute-start
  14.7 2.7 collective-permute-done
  22.2 35.6 %all_to_all.4 = bf16[8,32,2048]{2,1,0:T(8,128)(2,1)S(1)} all-to-all(bf16[8,32,2048]{2,1,0:T(8,128)(2,1)S(1)} %copy.36), channel_id=1, replica_groups=mesh['chan'=8,'tm'=64] {'chan'}, dimensions={0} | all-to-all | bytes 2097152 | tf_op jit(solution)/shard_map/all_to_all | solution.py:67
  62.3 125.6 %all-reduce.3 = (f32[64]{0:T(128)S(1)}, f32[64]{0:T(128)S(1)}) all-reduce(f32[64]{0:T(128)S(1)} %fusion.66, f32[64]{0:T(128)S(1)} %dynamic-update-slice.12), channel_id=2, replica_groups=mesh['chan'=8,'tm'=64] {'tm'}, use_global_device_ids=true, to_apply=%add.1 | all-reduce | flops 128 | bytes 1024
  189.0 237.8 %while.18 = (s32[]{:T(128)}, f32[1,256,256]{2,1,0:T(8,128)S(1)}, f32[1]{0:T(128)}, s32[]{:T(128)}, f32[64,1]{0,1:T(1,128)S(1)}, /*index=5*/f32[64,1,256,256]{3,2...) while((s32[]{:T(128)}, f32[1,256,256]{2,1,0:T(8,128)S(1)}, f32[1]{0:T(128)}, s32[]{:T(128)}, ...), condition=%wide.region_1.2_spmd.clone, body=%wide.region_0.1_spmd.clone.sunk | while | flops 262151 | bytes 786610 | solution.py:25
  189.7 1.7 fusion.81
  193.5 1.7 fusion.81
  197.3 1.7 fusion.81
  201.0 1.7 fusion.81
  204.8 1.7 fusion.81
  208.6 1.7 fusion.81
  212.4 1.7 fusion.81
  216.1 1.7 fusion.81
  219.9 1.7 fusion.81
  223.7 1.7 fusion.81
  227.5 1.7 fusion.81
  235.0 1.7 fusion.81
  257.7 1.7 fusion.81
  280.3 1.7 fusion.81
  306.7 1.7 fusion.81
  329.4 1.7 fusion.81
  352.0 1.7 fusion.81
  378.4 1.7 fusion.81
  401.1 1.7 fusion.81
  423.7 1.7 fusion.81
  429.0 11.7 %custom-call.16 = f32[1,128,128]{2,1,0:T(8,128)S(1)} custom-call(f32[1,128,128]{2,1,0:T(8,128)S(1)} %cholesky.114), custom_call_target="Cholesky" | custom-call | tf_op jit(solution)/shard_map/jit(cholesky)/cholesky | solution.py:83
  440.8 9.8 %custom-call.17 = f32[1,1,128,128]{2,3,1,0:T(8,128)S(1)} custom-call(f32[1,1,128,128]{3,2,1,0:T(8,128)S(1)} %get-tuple-element.223), custom_call_target="InvertDiagBlocksLowerTriangular" | custom-call | tf_op jit(solution)/shard_map/jit(cholesky)/cholesky | solution.py:83
  451.1 11.7 %custom-call.18 = f32[1,128,128]{2,1,0:T(8,128)S(1)} custom-call(f32[1,128,128]{2,1,0:T(8,128)S(1)} %fusion.13), custom_call_target="Cholesky" | custom-call | tf_op jit(solution)/shard_map/jit(cholesky)/cholesky | solution.py:83
  465.6 4.0 while.17
  469.5 19.9 %custom-call.19 = f32[1,2,128,128]{2,3,1,0:T(8,128)S(1)} custom-call(f32[1,2,128,128]{3,2,1,0:T(8,128)S(1)} %bitcast.227), custom_call_target="InvertDiagBlocksLowerTriangular" | custom-call | tf_op jit(solution)/shard_map/triangular_solve | solution.py:85
  490.3 2.0 fusion.9
  (166 shorter events, 136.6 us)
Async XLA Ops:
  6.5 6.9 %copy-start = (bf16[8,2,16,2048]{3,2,1,0:T(8,128)(2,1)S(1)}, bf16[8,2,16,2048]{3,2,1,0:T(8,128)(2,1)}, u32[]{:S(2)}) copy-start(bf16[8,2,16,2048]{3,2,1,0:T(8,128)(2,1)} %param.5) | copy-start | bytes 3145732
  6.5 6.8 %copy-start.1 = (f32[64]{0:T(128)S(1)}, f32[64]{0:T(128)}, u32[]{:S(2)}) copy-start(f32[64]{0:T(128)} %param.6) | copy-start | bytes 772
  6.5 182.5 %all-gather.4.cloned.1.call-start = ((), (), s32[]{:S(2)}) async-start(), calls=%async_computation.1 | async-start | bytes 17039360 | tf_op jit(solution)/shard_map/all_gather | solution.py:16
  8.5 8.9 %collective-permute-start = (bf16[8,2,16,7]{3,0,1,2:T(8,128)(2,1)S(1)}, bf16[8,2,16,7]{3,0,1,2:T(8,128)(2,1)S(1)}, u32[]{:S(2)}, u32[]{:S(2)}) collective-permute-start(bf16[8,2,16,7]{3,0,1,2:T(8,128)(2,1)S(1)} %slice.121), channel_id=1, source_target_pairs={{0,1},{1,2},{2,3},{3,4},{4,5},{5,6},{6,7},{7,8},{8,9},{9,10},{10,1... | collective-permute-start | bytes 10760 | tf_op jit(solution)/shard_map/ppermute | solution.py:11
Sparse Core Ops, SparseCore 0:
  59.1 101.0 all-gather.3
where the time goes:
time: 507 us; the launch traced here: 499 us
  other arithmetic  167 us (33%)
  blocking collectives  161 us (32%)
  loops' own time  85.9 us (17%)
  local copies, waits for them, and re-layouts  52.1 us (10%)
  between operations  16.3 us (3%)
  matrix products  9.79 us (2%)
    unnamed x1, blocking collectives  126 us
    select_n x63, other arithmetic, hop(): jnp.where(position < mine, new, old)  110 us
    another operation x1, loops' own time, carried_in(): return lax.fori_loop(0, count - 1, hop, total)  85.8 us
    dynamic_slice x63, local copies, waits for them, and re-layouts, hop(): longer = join(total, jax.tree.map(lambda part: part[position], pieces))  42 us
    all_to_all x1, blocking collectives, per_device(): lax.all_to_all(spectrum_rows, 'chan', split_axis=0, concat_axis=1, tiled=...  35.6 us
    another operation x7, other arithmetic, per_device(): factor_low = jnp.linalg.cholesky(moment / weight_sum[:, None, None])  34.6 us
    another operation x3, other arithmetic, per_device(): lax.linalg.triangular_solve(factor_low, identity_m, left_side=True, lower...  19.9 us
  transfers between devices with their start and end apart: 2, of which 1 were waited for; matrix products, arithmetic and copies ran while one was open for 1% of the time, Pallas kernels for 0%

commit v1 on v0

--- a/solution.py
+++ b/solution.py
@@ -64,7 +64,12 @@
     spectrum_rows = branch_sum.reshape(filter_branches, local_antenna_count * 2, frame_rows).astype(
         jnp.bfloat16
     )
-    turned = lax.all_to_all(spectrum_rows, "chan", split_axis=0, concat_axis=1, tiled=True)
+    turned = jnp.concatenate(
+        lax.all_to_all(
+            jnp.stack(jnp.split(spectrum_rows, lax.axis_size("chan"), axis=0)), "chan", 0, 0
+        ),
+        axis=1,
+    )
     channels_per_device = turned.shape[0]
     col_count = turned.shape[1]
     gram_now = jnp.einsum("cif,cjf->cij", turned, turned, preferred_element_type=jnp.float32)

time: 507 us -> 484 us (0.955)
  other arithmetic: 167 us -> 158 us
  loops' own time: 85.9 us -> 77 us
    another operation x1, loops' own time: 85.8 us -> 77 us  [carried_in(): return lax.fori_loop(0, count - 1, hop, total)]
    select_n x63, other arithmetic: 110 us -> 101 us  [hop(): jnp.where(position < mine, new, old)]
where the time goes in v1:
time: 484 us; the launch traced here: 480 us
  blocking collectives  161 us (33%)
  other arithmetic  158 us (33%)
  loops' own time  77 us (16%)
  local copies, waits for them, and re-layouts  50.5 us (10%)
  between operations  16.4 us (3%)
  matrix products  9.78 us (2%)
    unnamed x1, blocking collectives  125 us
    select_n x63, other arithmetic, hop(): jnp.where(position < mine, new, old)  101 us
    another operation x1, loops' own time, carried_in(): return lax.fori_loop(0, count - 1, hop, total)  77 us
    dynamic_slice x63, local copies, waits for them, and re-layouts, hop(): longer = join(total, jax.tree.map(lambda part: part[position], pieces))  37 us
    all_to_all x1, blocking collectives, per_device(): lax.all_to_all(jnp.stack(jnp.split(spectrum_rows, lax.axis_size('chan'),...  35.6 us
    another operation x7, other arithmetic, per_device(): factor_low = jnp.linalg.cholesky(moment / weight_sum[:, None, None])  34.6 us
    another operation x3, other arithmetic, per_device(): lax.linalg.triangular_solve(factor_low, identity_m, left_side=True, lower...  19.9 us
  transfers between devices with their start and end apart: 2, of which 1 were waited for; matrix products, arithmetic and copies ran while one was open for 1% of the time, Pallas kernels for 0%

profile of v1, /device:TPU:1, one launch (start us, length us, event | category | flops | bytes accessed | tf_op | source)
XLA Modules:
  0.0 479.8 jit_solution(10140956813355022432)
XLA Ops:
  6.5 1.9 copy.13
  8.5 4.6 collective-permute-start
  14.7 2.7 collective-permute-done
  21.5 1.8 fusion.69
  25.7 35.6 %all_to_all.5 = bf16[8,1,32,2048]{3,2,1,0:T(8,128)(2,1)S(1)} all-to-all(bf16[8,1,32,2048]{3,2,1,0:T(8,128)(2,1)S(1)} %constant_dynamic-update-slice_fusion), channel_id=1, replica_groups=mesh['chan'=8,'tm'=64] {'chan'}, dimensions={0} | all-to-all | bytes 2097152 | tf_op jit(solution)/shard_map/all_to_all | solution.py:68
  66.0 125.5 %all-reduce.3 = (f32[64]{0:T(128)S(1)}, f32[64]{0:T(128)S(1)}) all-reduce(f32[64]{0:T(128)S(1)} %fusion.66, f32[64]{0:T(128)S(1)} %dynamic-update-slice.12), channel_id=2, replica_groups=mesh['chan'=8,'tm'=64] {'tm'}, use_global_device_ids=true, to_apply=%add.1 | all-reduce | flops 128 | bytes 1024
  192.6 215.0 %while.18 = (s32[]{:T(128)}, f32[1,256,256]{2,1,0:T(8,128)S(1)}, f32[1]{0:T(128)}, s32[]{:T(128)}, f32[64,1]{0,1:T(1,128)S(1)}, /*index=5*/f32[64,1,256,256]{3,2...) while((s32[]{:T(128)}, f32[1,256,256]{2,1,0:T(8,128)S(1)}, f32[1]{0:T(128)}, s32[]{:T(128)}, ...), condition=%wide.region_1.2_spmd.clone, body=%wide.region_0.1_spmd.clone.sunk | while | flops 262151 | bytes 786610 | solution.py:25
  193.2 1.6 fusion.82
  196.7 1.6 fusion.82
  200.1 1.6 fusion.82
  203.5 1.6 fusion.82
  206.9 1.6 fusion.82
  210.3 1.6 fusion.82
  220.6 1.6 fusion.82
  224.0 1.6 fusion.82
  227.4 1.6 fusion.82
  230.8 1.6 fusion.82
  234.2 1.6 fusion.82
  237.6 1.6 fusion.82
  241.0 1.6 fusion.82
  244.4 1.6 fusion.82
  251.3 1.6 fusion.82
  254.7 1.6 fusion.82
  258.1 1.6 fusion.82
  261.5 1.6 fusion.82
  264.9 1.6 fusion.82
  409.9 11.7 %custom-call.16 = f32[1,128,128]{2,1,0:T(8,128)S(1)} custom-call(f32[1,128,128]{2,1,0:T(8,128)S(1)} %cholesky.114), custom_call_target="Cholesky" | custom-call | tf_op jit(solution)/shard_map/jit(cholesky)/cholesky | solution.py:88
  421.6 9.8 %custom-call.17 = f32[1,1,128,128]{2,3,1,0:T(8,128)S(1)} custom-call(f32[1,1,128,128]{3,2,1,0:T(8,128)S(1)} %get-tuple-element.217), custom_call_target="InvertDiagBlocksLowerTriangular" | custom-call | tf_op jit(solution)/shard_map/jit(cholesky)/cholesky | solution.py:88
  431.9 11.7 %custom-call.18 = f32[1,128,128]{2,1,0:T(8,128)S(1)} custom-call(f32[1,128,128]{2,1,0:T(8,128)S(1)} %fusion.13), custom_call_target="Cholesky" | custom-call | tf_op jit(solution)/shard_map/jit(cholesky)/cholesky | solution.py:88
  446.4 3.9 while.17
  450.3 19.9 %custom-call.19 = f32[1,2,128,128]{2,3,1,0:T(8,128)S(1)} custom-call(f32[1,2,128,128]{3,2,1,0:T(8,128)S(1)} %bitcast.225), custom_call_target="InvertDiagBlocksLowerTriangular" | custom-call | tf_op jit(solution)/shard_map/triangular_solve | solution.py:90
  471.0 2.0 fusion.9
  (189 shorter events, 128.9 us)
Async XLA Ops:
  6.5 6.9 %copy-start = (bf16[8,2,16,2048]{3,2,1,0:T(8,128)(2,1)S(1)}, bf16[8,2,16,2048]{3,2,1,0:T(8,128)(2,1)}, u32[]{:S(2)}) copy-start(bf16[8,2,16,2048]{3,2,1,0:T(8,128)(2,1)} %param.5) | copy-start | bytes 3145732
  6.5 6.8 %copy-start.1 = (f32[64]{0:T(128)S(1)}, f32[64]{0:T(128)}, u32[]{:S(2)}) copy-start(f32[64]{0:T(128)} %param.6) | copy-start | bytes 772
  6.5 186.1 %all-gather.4.cloned.1.call-start = ((), (), s32[]{:S(2)}) async-start(), calls=%async_computation.1 | async-start | bytes 17039360 | tf_op jit(solution)/shard_map/all_gather | solution.py:16
  8.5 8.9 %collective-permute-start = (bf16[8,2,16,7]{3,0,1,2:T(8,128)(2,1)S(1)}, bf16[8,2,16,7]{3,0,1,2:T(8,128)(2,1)S(1)}, u32[]{:S(2)}, u32[]{:S(2)}) collective-permute-start(bf16[8,2,16,7]{3,0,1,2:T(8,128)(2,1)S(1)} %slice.129), channel_id=1, source_target_pairs={{0,1},{1,2},{2,3},{3,4},{4,5},{5,6},{6,7},{7,8},{8,9},{9,10},{10,1... | collective-permute-start | bytes 10760 | tf_op jit(solution)/shard_map/ppermute | solution.py:11
Sparse Core Ops, SparseCore 0:
  62.5 100.9 all-gather.3
